TPU v7x, 32 devices: a whole 2x2x4 slice. The times are simulated.
32 devices in a mesh: groups: 2 (over x), wide: 16 (over z, y, core).
Axes of the slice: x: 2, y: 2, z: 4, core: 2. Of those that a mesh axis runs over, the one named last changes fastest.
Arguments:
- frames_in: bfloat16 [128, 256, 768], P(('groups', 'wide')), parts along dimension 0, may hold values from -5 to 5
- qkv_spatial: bfloat16 [768, 2304], replicated, may hold values from -6.5 to 6.5
- out_spatial: bfloat16 [768, 768], replicated, may hold values from -0.21875 to 0.21875
- qkv_temporal: bfloat16 [768, 2304], replicated, may hold values from -6.5 to 6.5
- out_temporal: bfloat16 [768, 768], replicated, may hold values from -0.21875 to 0.21875
Outputs:
- frames_out: bfloat16 [128, 256, 768], P(('groups', 'wide')), parts along dimension 0
There are 2 independent parts, one for each index of `groups`. A program takes and returns all parts, laid end to end along the dimension named above; an argument that names none is the same for every part. Nothing has to cross between parts.
All inputs are finite; a program needn't handle non-finite values.
Results may differ from a plain program's by a relative error of at most 0.008.
Values may be sent and summed in bfloat16 or wider, within the bound.
A program may use at most 128 MiB of HBM per device.

v0:
```python
import jax
import jax.numpy as jnp
from jax import lax
from jax.sharding import PartitionSpec as P

HEADS = 12
HEAD_DIM = 64


def normalize(tensor):
    floats = tensor.astype(jnp.float32)
    average = jnp.mean(floats, axis=-1, keepdims=True)
    centred = floats - average
    spread = jnp.mean(centred * centred, axis=-1, keepdims=True)
    return (centred * lax.rsqrt(spread + 1e-06)).astype(jnp.bfloat16)


def project(flat_rows, matrix):
    return jnp.dot(flat_rows, matrix, preferred_element_type=jnp.float32)


def attend(projected, score_form, mix_form):
    leading = projected.shape[:-1]
    split = projected.reshape(leading + (3, HEADS, HEAD_DIM))
    queries = split[..., 0, :, :]
    key_part = split[..., 1, :, :]
    values = split[..., 2, :, :]
    scores = jnp.einsum(
        score_form, queries, key_part, preferred_element_type=jnp.float32
    ) * HEAD_DIM ** (-0.5)
    weights = jax.nn.softmax(scores, axis=-1).astype(jnp.bfloat16)
    mixed = jnp.einsum(mix_form, weights, values, preferred_element_type=jnp.float32)
    return mixed.reshape(leading + (HEADS * HEAD_DIM,)).astype(jnp.bfloat16)


def attend_time(received):
    frame_total, single, item_count, columns = received.shape
    sequences = received.reshape(frame_total, item_count, columns)
    result = attend(sequences, "qbhd,kbhd->bhqk", "bhqk,kbhd->qbhd")
    return result.reshape(frame_total, single, item_count, HEADS * HEAD_DIM)


def shards(frames_in, qkv_spatial, out_spatial, qkv_temporal, out_temporal):
    frame_count, patch_count, features = frames_in.shape
    wide_count = lax.axis_size("wide")
    per_group = patch_count // wide_count
    first = normalize(frames_in)
    proj_one = project(first.reshape(-1, features), qkv_spatial).astype(jnp.bfloat16)
    proj_one = proj_one.reshape(frame_count, patch_count, 3 * features)
    spatial = attend(proj_one, "bqhd,bkhd->bhqk", "bhqk,bkhd->bqhd")
    update = project(spatial.reshape(-1, features), out_spatial).reshape(
        frame_count, patch_count, features
    )
    middle = (frames_in.astype(jnp.float32) + update).astype(jnp.bfloat16)
    second = normalize(middle)
    grouped = second.reshape(frame_count, wide_count, per_group, features)
    received = lax.all_to_all(grouped, "wide", split_axis=1, concat_axis=0, tiled=True)
    frame_total, single, item_count, columns = received.shape
    local_proj = project(received.reshape(-1, columns), qkv_temporal).astype(jnp.bfloat16)
    local_proj = local_proj.reshape(frame_total, single, item_count, 3 * columns)
    temporal = attend_time(local_proj)
    returned = lax.all_to_all(temporal, "wide", split_axis=0, concat_axis=1, tiled=True)
    change = project(returned.reshape(-1, features), out_temporal).reshape(
        frame_count, patch_count, features
    )
    return (middle.astype(jnp.float32) + change).astype(jnp.bfloat16)


def solution(mesh):
    return jax.shard_map(
        shards,
        mesh=mesh,
        in_specs=(P(("groups", "wide"), None, None), P(), P(), P(), P()),
        out_specs=P(("groups", "wide"), None, None),
        check_vma=False,
    )
```

profile of v0, /device:TPU:1, one launch (start us, length us, event | category | flops | bytes accessed | tf_op | source)
XLA Modules:
  0.0 206.3 jit_solution(2839607701515157252)
XLA Ops:
  0.0 0.0 copy-start
  0.0 0.0 copy-start.2
  0.0 1.8 convert_reduce_fusion.1
  1.9 2.1 %fusion.16 = f32[4,256]{1,0:T(4,128)S(1)} fusion(bf16[4,256,768]{2,1,0:T(8,128)(2,1)} %param.5, f32[4,256]{1,0:T(4,128)S(1)} %broadcast_multiply_fusion.1), kind=kLoop, calls=%fused_computation.26 | loop fusion | flops 3144704 | bytes 1581056 | tf_op jit(solution)/shard_map/reduce_sum | solution.py:14
  4.0 0.0 copy-done.2
  4.0 0.4 fusion.17
  4.5 0.0 copy-done
  4.5 5.5 %convolution_convert_fusion.1 = bf16[1024,2304]{1,0:T(8,128)(2,1)} fusion(bf16[1024,768]{1,0:T(8,128)(2,1)S(1)} %bitcast.56, bf16[768,2304]{1,0:T(8,128)(2,1)S(1)} %copy-done), kind=kOutput, calls=%fused_computation.11 | convolution fusion | flops 3626237952 | bytes 9830400 | tf_op jit(solution)/shard_map/dot_general | solution.py:19
  10.0 6.6 %copy.29 = bf16[1024,2304]{0,1:T(8,128)(2,1)} copy(bf16[1024,2304]{1,0:T(8,128)(2,1)} %convolution_convert_fusion.1) | data formatting | bytes 9437184 | tf_op jit(solution)/shard_map/convert_element_type | solution.py:48
  16.6 8.9 %reshape_reshape.3 = bf16[4,256,3,12,64]{1,0,4,3,2:T(4,128)(2,1)} reshape(bf16[1024,2304]{0,1:T(8,128)(2,1)} %copy.29) | data formatting | bytes 9437184 | tf_op jit(solution)/shard_map/reshape;reshape | solution.py:24
  25.5 3.3 %fusion.35 = (bf16[4,256,1,12,64]{1,0,4,3,2:T(4,128)(2,1)S(1)}, bf16[4,256,1,12,64]{1,0,4,3,2:T(4,128)(2,1)S(1)}, bf16[4,256,1,12,64]{1,0,4,3,2:T(4,128)(2,1)S(1)}) fusion(bf16[4,256,3,12,64]{1,0,4,3,2:T(4,128)(2,1)} %reshape_reshape.3), kind=kLoop, calls=%fused_computation.52 | loop fusion | bytes 9437184 | tf_op jit(solution)/shard_map/slice | solution.py:27
  28.9 6.4 %fusion.29 = f32[4,12,256,256]{2,3,1,0:T(8,128)} fusion(bf16[4,256,1,12,64]{1,0,4,3,2:T(4,128)(2,1)S(1)} %get-tuple-element.10, bf16[4,256,1,12,64]{1,0,4,3,2:T(4,128)(2,1)S(1)} %get-tuple-element.9), kind=kOutput, calls=%fused_computation.40 | convolution fusion | flops 402653184 | bytes 15728640 | tf_op jit(solution)/shard_map/bqhd,bkhd->bhqk/dot_general | solution.py:28
  35.3 15.8 %fusion.36 = (f32[4,12,256]{2,1,0:T(8,128)S(1)}, f32[4,12,256,256]{2,3,1,0:T(8,128)}) fusion(f32[4,12,256,256]{2,3,1,0:T(8,128)} %fusion.29), kind=kOutput, calls=%fused_computation.53 | output fusion | flops 12583167 | bytes 25214976 | tf_op jit(solution)/shard_map/sub | solution.py:31
  51.1 0.0 copy-start.3
  51.1 0.0 copy-start.7
  51.1 5.8 %fusion.28 = bf16[4,12,64,256]{3,2,1,0:T(8,128)(2,1)S(1)} fusion(f32[4,12,256,256]{2,3,1,0:T(8,128)} %get-tuple-element.12, f32[4,12,256]{2,1,0:T(8,128)S(1)} %get-tuple-element.11, bf16[4,256,1,12,64]{1,0,4,3,2:T(4,128)(2,1)S(1)} %get-tuple-element.8), kind=kOutput, calls=%fused_computation.38 | convolution fusion | flops 409731072 | bytes 15777792 | tf_op jit(solution)/shard_map/bhqk,bkhd->bqhd/dot_general | solution.py:32
  56.9 0.0 copy-done.3
  56.9 0.0 copy-done.7
  56.9 1.6 convert_reduce_fusion
  58.5 0.0 copy-start.4
  58.5 0.6 fusion.14
  59.1 0.4 fusion.15
  59.5 0.0 copy-start.6
  59.6 0.2 copy.35
  59.7 0.0 copy-done.4
  59.7 43.9 %all_to_all.30 = bf16[4,16,16,768]{3,2,0,1:T(8,128)(2,1)S(1)} all-to-all(bf16[4,16,16,768]{3,2,0,1:T(8,128)(2,1)S(1)} %copy.35), channel_id=1, replica_groups=mesh['groups'=2,'wide'=16] {'wide'}, dimensions={1} | all-to-all | bytes 3145728 | tf_op jit(solution)/shard_map/all_to_all | solution.py:57
  103.6 0.0 copy-done.6
  103.6 5.4 %convolution_convert_fusion = bf16[1024,2304]{1,0:T(8,128)(2,1)} fusion(bf16[1024,768]{1,0:T(8,128)(2,1)S(1)} %bitcast.58, bf16[768,2304]{1,0:T(8,128)(2,1)S(1)} %copy-done.6), kind=kOutput, calls=%fused_computation.10 | convolution fusion | flops 3626237952 | bytes 9830400 | tf_op jit(solution)/shard_map/dot_general | solution.py:19
  109.0 14.9 %reshape_reshape_reshape.3 = bf16[64,16,3,12,64]{4,3,2,1,0:T(8,128)(2,1)} reshape(bf16[1024,2304]{1,0:T(8,128)(2,1)} %convolution_convert_fusion) | data formatting | bytes 9437184 | tf_op jit(solution)/shard_map/reshape;reshape;reshape | solution.py:24
  124.0 9.2 %fusion.34 = (bf16[64,16,1,12,64]{4,3,2,1,0:T(8,128)(2,1)}, bf16[64,16,1,12,64]{4,3,2,1,0:T(8,128)(2,1)}, bf16[64,16,1,12,64]{4,3,2,1,0:T(8,128)(2,1)}) fusion(bf16[64,16,3,12,64]{4,3,2,1,0:T(8,128)(2,1)} %reshape_reshape_reshape.3), kind=kLoop, calls=%fused_computation.51 | loop fusion | bytes 9437184 | tf_op jit(solution)/shard_map/slice | solution.py:27
  133.2 6.4 %copy.48 = bf16[64,16,1,12,64]{0,4,3,1,2:T(8,128)(2,1)S(1)} copy(bf16[64,16,1,12,64]{4,3,2,1,0:T(8,128)(2,1)} %get-tuple-element.5) | data formatting | bytes 3145728
  139.7 7.2 %fusion.21 = f32[16,12,64,64]{2,3,1,0:T(8,128)S(1)} fusion(bf16[64,16,1,12,64]{4,3,2,1,0:T(8,128)(2,1)} %get-tuple-element.6, bf16[64,16,1,12,64]{4,3,2,1,0:T(8,128)(2,1)} %get-tuple-element.7), kind=kOutput, calls=%fused_computation.32 | convolution fusion | flops 100663296 | bytes 6291456 | tf_op jit(solution)/shard_map/qbhd,kbhd->bhqk/dot_general | solution.py:28
  146.9 9.2 %fusion.37 = (f32[16,12,64]{2,1,0:T(8,128)S(1)}, f32[16,12,64,64]{2,3,1,0:T(8,128)S(1)}) fusion(f32[16,12,64,64]{2,3,1,0:T(8,128)S(1)} %fusion.21), kind=kOutput, calls=%fused_computation.54 | output fusion | flops 3145791 | bytes 6340608 | tf_op jit(solution)/shard_map/sub | solution.py:31
  156.0 2.6 %fusion.25 = bf16[16,12,64,64]{3,2,1,0:T(8,128)(2,1)} fusion(f32[16,12,64,64]{2,3,1,0:T(8,128)S(1)} %get-tuple-element.16, f32[16,12,64]{2,1,0:T(8,128)S(1)} %get-tuple-element.15, bf16[64,16,1,12,64]{0,4,3,1,2:T(8,128)(2,1)S(1)} %copy.48), kind=kOutput, calls=%fused_computation.37 | convolution fusion | flops 103022592 | bytes 6340608 | tf_op jit(solution)/shard_map/bhqk,kbhd->qbhd/dot_general | solution.py:32
  158.7 3.9 %copy.40 = bf16[64,1,16,768]{3,2,1,0:T(8,128)(2,1)S(1)} copy(bf16[64,1,16,768]{0,3,2,1:T(8,128)(2,1)} %bitcast.55) | data formatting | bytes 3145728 | tf_op jit(solution)/shard_map/convert_element_type | solution.py:33
  162.6 0.0 copy-start.5
  162.6 0.0 copy-start.8
  162.6 41.0 %all_to_all.31 = bf16[64,1,16,768]{3,2,1,0:T(8,128)(2,1)S(1)} all-to-all(bf16[64,1,16,768]{3,2,1,0:T(8,128)(2,1)S(1)} %copy.40), channel_id=1, replica_groups=mesh['groups'=2,'wide'=16] {'wide'}, dimensions={0} | all-to-all | bytes 3145728 | tf_op jit(solution)/shard_map/all_to_all | solution.py:62
  203.6 0.1 copy.41
  203.8 0.0 copy-start.1
  203.8 0.0 copy-done.5
  203.8 0.0 copy-done.8
  203.8 2.5 %fusion.19 = bf16[4,256,768]{2,1,0:T(8,128)(2,1)} fusion(bf16[4,256,768]{2,1,0:T(8,128)(2,1)S(1)} %copy-done.5, bf16[4,256,768]{2,1,0:T(8,128)(2,1)S(1)} %bitcast.57, bf16[768,768]{1,0:T(8,128)(2,1)S(1)} %copy-done.8), kind=kOutput, calls=%fused_computation.29 | convolution fusion | flops 1210318848 | bytes 5898240 | tf_op jit(solution)/shard_map/dot_general | solution.py:19
  206.3 0.0 copy-done.1
  (4 shorter events, 0.0 us)
Async XLA Ops:
  0.0 4.5 %copy-start = (bf16[768,2304]{1,0:T(8,128)(2,1)S(1)}, bf16[768,2304]{1,0:T(8,128)(2,1)}, u32[]{:S(2)}) copy-start(bf16[768,2304]{1,0:T(8,128)(2,1)} %param.6) | copy-start | bytes 10616836
  0.0 4.0 %copy-start.2 = (bf16[4,256,768]{2,1,0:T(8,128)(2,1)S(1)}, bf16[4,256,768]{2,1,0:T(8,128)(2,1)}, u32[]{:S(2)}) copy-start(bf16[4,256,768]{2,1,0:T(8,128)(2,1)} %param.5) | copy-start | bytes 4718596
  51.1 5.8 %copy-start.3 = (bf16[4,256,768]{2,1,0:T(8,128)(2,1)S(1)}, bf16[4,256,768]{2,1,0:T(8,128)(2,1)}, u32[]{:S(2)}) copy-start(bf16[4,256,768]{2,1,0:T(8,128)(2,1)} %param.5) | copy-start | bytes 4718596
  51.1 5.8 %copy-start.7 = (bf16[768,768]{1,0:T(8,128)(2,1)S(1)}, bf16[768,768]{1,0:T(8,128)(2,1)}, u32[]{:S(2)}) copy-start(bf16[768,768]{1,0:T(8,128)(2,1)} %param.7) | copy-start | bytes 3538948
  58.5 1.2 copy-start.4
  59.5 44.1 %copy-start.6 = (bf16[768,2304]{1,0:T(8,128)(2,1)S(1)}, bf16[768,2304]{1,0:T(8,128)(2,1)}, u32[]{:S(2)}) copy-start(bf16[768,2304]{1,0:T(8,128)(2,1)} %param.8) | copy-start | bytes 10616836
  162.6 41.2 %copy-start.5 = (bf16[4,256,768]{2,1,0:T(8,128)(2,1)S(1)}, bf16[4,256,768]{2,1,0:T(8,128)(2,1)}, u32[]{:S(2)}) copy-start(bf16[4,256,768]{2,1,0:T(8,128)(2,1)} %copy-done.4) | copy-start | bytes 4718596
  162.6 41.2 %copy-start.8 = (bf16[768,768]{1,0:T(8,128)(2,1)S(1)}, bf16[768,768]{1,0:T(8,128)(2,1)}, u32[]{:S(2)}) copy-start(bf16[768,768]{1,0:T(8,128)(2,1)} %param.9) | copy-start | bytes 3538948
  203.8 2.6 %copy-start.1 = (bf16[768,2304]{1,0:T(8,128)(2,1)S(1)}, bf16[768,2304]{1,0:T(8,128)(2,1)}, u32[]{:S(2)}) copy-start(bf16[768,2304]{1,0:T(8,128)(2,1)} %param.6) | copy-start | bytes 10616836
where the time goes:
time: 207 us; the launch traced here: 206 us
  blocking collectives  84.9 us (41%)
  local copies, waits for them, and re-layouts  53.7 us (26%)
  matrix products  37.1 us (18%)
  other arithmetic  30.4 us (15%)
    all_to_all x1, blocking collectives, shards(): lax.all_to_all(grouped, 'wide', split_axis=1, concat_axis=0, tiled=True)  43.9 us
    all_to_all x1, blocking collectives, shards(): lax.all_to_all(temporal, 'wide', split_axis=0, concat_axis=1, tiled=True)  41 us
    sub x2, other arithmetic, attend(): weights = jax.nn.softmax(scores, axis=-1).astype(jnp.bfloat16)  24.9 us
    another operation x2, local copies, waits for them, and re-layouts, attend(): split = projected.reshape(leading + (3, HEADS, HEAD_DIM))  23.9 us
    dot_general x4, matrix products, project(): return jnp.dot(flat_rows, matrix, preferred_element_type=jnp.float32)  15.1 us
    dot_general x2, matrix products, attend(): jnp.einsum(score_form, queries, key_part, preferred_element_type=jnp.floa...  13.6 us
    slice x2, local copies, waits for them, and re-layouts, attend(): values = split[..., 2, :, :]  12.6 us
    dot_general x2, matrix products, attend(): jnp.einsum(mix_form, weights, values, preferred_element_type=jnp.float32)  8.47 us

commit v1 on v0

--- a/solution.py
+++ b/solution.py
@@ -59,7 +59,10 @@
     local_proj = project(received.reshape(-1, columns), qkv_temporal).astype(jnp.bfloat16)
     local_proj = local_proj.reshape(frame_total, single, item_count, 3 * columns)
     temporal = attend_time(local_proj)
-    returned = lax.all_to_all(temporal, "wide", split_axis=0, concat_axis=1, tiled=True)
+    returned = jnp.concatenate(
+        lax.all_to_all(jnp.stack(jnp.split(temporal, lax.axis_size("wide"), axis=0)), "wide", 0, 0),
+        axis=1,
+    )
     change = project(returned.reshape(-1, features), out_temporal).reshape(
         frame_count, patch_count, features
     )

time: 207 us -> 199 us (0.961)
  local copies, waits for them, and re-layouts: 53.7 us -> 49.1 us
  matrix products: 37.1 us -> 34.7 us
    unnamed x19 -> x57, local copies, waits for them, and re-layouts: 6.49 us -> 2.21 us
    split x0 -> x17, local copies, waits for them, and re-layouts: none -> 4.17 us  [shards(): jnp.split(temporal, lax.axis_size('wide'), axis=0)]
    convert_element_type x1 -> x0, local copies, waits for them, and re-layouts: 3.89 us -> none  [attend(): return mixed.reshape(leading + (HEADS * HEAD_DIM,)).astype(jnp.bfloat16)]
    dot_general x2, matrix products: 13.6 us -> 10.1 us  [attend(): jnp.einsum(score_form, queries, key_part, preferred_element_type=jnp.floa...]
    slice x2, local copies, waits for them, and re-layouts: 12.6 us -> 9.24 us  [attend(): values = split[..., 2, :, :]]
    another operation x0 -> x17, local copies, waits for them, and re-layouts: none -> 2.67 us  [shards(): jnp.stack(jnp.split(temporal, lax.axis_size('wide'), axis=0))]
where the time goes in v1:
time: 199 us; the launch traced here: 198 us
  blocking collectives  84.7 us (43%)
  local copies, waits for them, and re-layouts  49.1 us (25%)
  matrix products  34.7 us (17%)
  other arithmetic  29.1 us (15%)
    all_to_all x1, blocking collectives, shards(): lax.all_to_all(grouped, 'wide', split_axis=1, concat_axis=0, tiled=True)  43.9 us
    all_to_all x1, blocking collectives, shards(): lax.all_to_all(jnp.stack(jnp.split(temporal, lax.axis_size('wide'), axis=...  40.8 us
    sub x2, other arithmetic, attend(): weights = jax.nn.softmax(scores, axis=-1).astype(jnp.bfloat16)  25.1 us
    another operation x2, local copies, waits for them, and re-layouts, attend(): split = projected.reshape(leading + (3, HEADS, HEAD_DIM))  23.8 us
    dot_general x4, matrix products, project(): return jnp.dot(flat_rows, matrix, preferred_element_type=jnp.float32)  15 us
    dot_general x2, matrix products, attend(): jnp.einsum(score_form, queries, key_part, preferred_element_type=jnp.floa...  10.1 us
    dot_general x2, matrix products, attend(): jnp.einsum(mix_form, weights, values, preferred_element_type=jnp.float32)  9.57 us
    slice x2, local copies, waits for them, and re-layouts, attend(): values = split[..., 2, :, :]  9.24 us

profile of v1, /device:TPU:1, one launch (start us, length us, event | category | flops | bytes accessed | tf_op | source)
XLA Modules:
  0.0 198.1 jit_solution(14481359140444804451)
XLA Ops:
  0.0 1.8 convert_reduce_fusion.1
  1.9 0.2 copy-done.2
  2.0 0.6 fusion.16
  2.6 0.4 fusion.17
  3.1 5.5 %convolution_convert_fusion.1 = bf16[1024,2304]{1,0:T(8,128)(2,1)} fusion(bf16[1024,768]{1,0:T(8,128)(2,1)S(1)} %bitcast.52, bf16[768,2304]{1,0:T(8,128)(2,1)S(1)} %copy-done), kind=kOutput, calls=%fused_computation.11 | convolution fusion | flops 3626237952 | bytes 9830400 | tf_op jit(solution)/shard_map/dot_general | solution.py:19
  8.6 6.6 %copy.15 = bf16[1024,2304]{0,1:T(8,128)(2,1)} copy(bf16[1024,2304]{1,0:T(8,128)(2,1)} %convolution_convert_fusion.1) | data formatting | bytes 9437184 | tf_op jit(solution)/shard_map/convert_element_type | solution.py:48
  15.3 8.9 %reshape_reshape.4 = bf16[4,256,3,12,64]{1,0,4,3,2:T(4,128)(2,1)} reshape(bf16[1024,2304]{0,1:T(8,128)(2,1)} %copy.15) | data formatting | bytes 9437184 | tf_op jit(solution)/shard_map/reshape;reshape | solution.py:24
  24.2 3.3 %fusion.31 = (bf16[4,256,1,12,64]{1,0,4,3,2:T(4,128)(2,1)S(1)}, bf16[4,256,1,12,64]{1,0,4,3,2:T(4,128)(2,1)S(1)}, bf16[4,256,1,12,64]{1,0,4,3,2:T(4,128)(2,1)S(1)}) fusion(bf16[4,256,3,12,64]{1,0,4,3,2:T(4,128)(2,1)} %reshape_reshape.4), kind=kLoop, calls=%fused_computation.68 | loop fusion | bytes 9437184 | tf_op jit(solution)/shard_map/slice | solution.py:27
  27.5 6.4 %fusion.25 = f32[4,12,256,256]{2,3,1,0:T(8,128)} fusion(bf16[4,256,1,12,64]{1,0,4,3,2:T(4,128)(2,1)S(1)} %get-tuple-element.10, bf16[4,256,1,12,64]{1,0,4,3,2:T(4,128)(2,1)S(1)} %get-tuple-element.9), kind=kOutput, calls=%fused_computation.40 | convolution fusion | flops 402653184 | bytes 15728640 | tf_op jit(solution)/shard_map/bqhd,bkhd->bhqk/dot_general | solution.py:28
  33.9 15.8 %fusion.33 = (f32[4,12,256]{2,1,0:T(8,128)S(1)}, f32[4,12,256,256]{2,3,1,0:T(8,128)}) fusion(f32[4,12,256,256]{2,3,1,0:T(8,128)} %fusion.25), kind=kOutput, calls=%fused_computation.70 | output fusion | flops 12583167 | bytes 25214976 | tf_op jit(solution)/shard_map/sub | solution.py:31
  49.7 5.8 %fusion.24 = bf16[4,12,64,256]{3,2,1,0:T(8,128)(2,1)S(1)} fusion(f32[4,12,256,256]{2,3,1,0:T(8,128)} %get-tuple-element.28, f32[4,12,256]{2,1,0:T(8,128)S(1)} %get-tuple-element.27, bf16[4,256,1,12,64]{1,0,4,3,2:T(4,128)(2,1)S(1)} %get-tuple-element.8), kind=kOutput, calls=%fused_computation.38 | convolution fusion | flops 409731072 | bytes 15777792 | tf_op jit(solution)/shard_map/bhqk,bkhd->bqhd/dot_general | solution.py:32
  55.5 1.6 convert_reduce_fusion
  57.1 0.6 fusion.14
  57.7 0.4 fusion.15
  58.2 0.1 copy-done.4
  58.2 0.2 copy.21
  58.4 43.9 %all_to_all.20 = bf16[4,16,16,768]{3,2,0,1:T(8,128)(2,1)S(1)} all-to-all(bf16[4,16,16,768]{3,2,0,1:T(8,128)(2,1)S(1)} %copy.21), channel_id=1, replica_groups=mesh['groups'=2,'wide'=16] {'wide'}, dimensions={1} | all-to-all | bytes 3145728 | tf_op jit(solution)/shard_map/all_to_all | solution.py:57
  102.3 5.4 %convolution_convert_fusion = bf16[1024,2304]{1,0:T(8,128)(2,1)} fusion(bf16[1024,768]{1,0:T(8,128)(2,1)S(1)} %bitcast.54, bf16[768,2304]{1,0:T(8,128)(2,1)S(1)} %copy-done.18), kind=kOutput, calls=%fused_computation.10 | convolution fusion | flops 3626237952 | bytes 9830400 | tf_op jit(solution)/shard_map/dot_general | solution.py:19
  107.7 14.9 %reshape_reshape_reshape.3 = bf16[64,16,3,12,64]{4,3,2,1,0:T(8,128)(2,1)} reshape(bf16[1024,2304]{1,0:T(8,128)(2,1)} %convolution_convert_fusion) | data formatting | bytes 9437184 | tf_op jit(solution)/shard_map/reshape;reshape;reshape | solution.py:24
  122.6 5.9 %fusion.30 = (bf16[64,16,1,12,64]{4,3,2,1,0:T(8,128)(2,1)S(1)}, bf16[64,16,1,12,64]{4,3,2,1,0:T(8,128)(2,1)S(1)}, bf16[64,16,1,12,64]{4,3,2,1,0:T(8,128)(2,1)S(1)}) fusion(bf16[64,16,3,12,64]{4,3,2,1,0:T(8,128)(2,1)} %reshape_reshape_reshape.3), kind=kLoop, calls=%fused_computation.67 | loop fusion | bytes 9437184 | tf_op jit(solution)/shard_map/slice | solution.py:27
  128.5 3.7 %fusion.21 = f32[16,12,64,64]{2,3,1,0:T(8,128)S(1)} fusion(bf16[64,16,1,12,64]{4,3,2,1,0:T(8,128)(2,1)S(1)} %get-tuple-element.7, bf16[64,16,1,12,64]{4,3,2,1,0:T(8,128)(2,1)S(1)} %get-tuple-element.6), kind=kOutput, calls=%fused_computation.32 | convolution fusion | flops 100663296 | bytes 6291456 | tf_op jit(solution)/shard_map/qbhd,kbhd->bhqk/dot_general | solution.py:28
  132.3 9.4 %fusion.34 = (f32[16,12,64]{2,1,0:T(8,128)S(1)}, f32[16,12,64,64]{2,3,1,0:T(8,128)S(1)}) fusion(f32[16,12,64,64]{2,3,1,0:T(8,128)S(1)} %fusion.21), kind=kOutput, calls=%fused_computation.71 | output fusion | flops 3145791 | bytes 6340608 | tf_op jit(solution)/shard_map/sub | solution.py:31
  141.7 3.7 %convert_bitcast_fusion = bf16[64,16,12,64]{3,0,2,1:T(8,128)(2,1)S(1)} fusion(f32[16,12,64,64]{2,3,1,0:T(8,128)S(1)} %get-tuple-element.32, f32[16,12,64]{2,1,0:T(8,128)S(1)} %get-tuple-element.31, bf16[64,16,1,12,64]{4,3,2,1,0:T(8,128)(2,1)S(1)} %get-tuple-element.5), kind=kOutput, calls=%fused_computation.35 | convolution fusion | flops 103022592 | bytes 6340608 | tf_op jit(solution)/shard_map/bhqk,kbhd->qbhd/dot_general | solution.py:32
  145.4 2.5 %fusion.32 = (bf16[4,16,12,64]{3,0,2,1:T(4,128)(2,1)S(1)}, bf16[4,16,12,64]{3,0,2,1:T(4,128)(2,1)}, bf16[4,16,12,64]{3,0,2,1:T(4,128)(2,1)}, bf16[4,16,12,64]{3,...) fusion(bf16[64,16,12,64]{3,0,2,1:T(8,128)(2,1)S(1)} %convert_bi, ...), kind=kLoop, calls=%fused_computation.69 | loop fusion | bytes 3145728 | tf_op jit(solution)/shard_map/split | solution.py:63
  147.9 0.2 stack.66
  148.1 1.0 copy.40
  149.2 0.2 stack.65
  149.4 0.2 stack.64
  149.6 0.2 stack.63
  149.9 0.2 stack.62
  150.1 0.2 stack.61
  150.4 0.2 stack.60
  150.6 0.2 stack.59
  150.9 0.2 stack.58
  151.0 0.0 copy-done.10
  151.1 0.2 stack.57
  151.4 0.2 stack.56
  151.6 0.2 stack.55
  151.8 0.2 stack.54
  152.0 0.0 copy-done.6
  152.1 0.2 stack.53
  152.3 0.2 stack.52
  152.5 0.2 stack.51
  153.0 40.8 %all_to_all.21 = bf16[16,4,1,16,768]{4,3,1,2,0:T(8,128)(2,1)S(1)} all-to-all(bf16[16,4,1,16,768]{4,3,1,2,0:T(8,128)(2,1)S(1)} %constant_dynamic-update-slice_fusion), channel_id=1, replica_groups=mesh['groups'=2,'wide'=16] {'wide'}, dimensions={0} | all-to-all | bytes 3145728 | tf_op jit(solution)/shard_map/all_to_all | solution.py:63
  193.8 0.1 copy.42
  193.9 1.3 copy-done.5
  195.2 0.3 copy-done.20
  195.5 2.5 %fusion.19 = bf16[4,256,768]{2,1,0:T(8,128)(2,1)} fusion(bf16[4,256,768]{2,1,0:T(8,128)(2,1)S(1)} %copy-done.5, bf16[4,256,768]{2,1,0:T(8,128)(2,1)S(1)} %bitcast.53, bf16[768,768]{1,0:T(8,128)(2,1)S(1)} %copy-done.20), kind=kOutput, calls=%fused_computation.29 | convolution fusion | flops 1210318848 | bytes 5898240 | tf_op jit(solution)/shard_map/dot_general | solution.py:19
  (71 shorter events, 1.0 us)
Async XLA Ops:
  0.0 3.1 %copy-start = (bf16[768,2304]{1,0:T(8,128)(2,1)S(1)}, bf16[768,2304]{1,0:T(8,128)(2,1)}, u32[]{:S(2)}) copy-start(bf16[768,2304]{1,0:T(8,128)(2,1)} %param.6) | copy-start | bytes 10616836
  0.0 2.0 %copy-start.2 = (bf16[4,256,768]{2,1,0:T(8,128)(2,1)S(1)}, bf16[4,256,768]{2,1,0:T(8,128)(2,1)}, u32[]{:S(2)}) copy-start(bf16[4,256,768]{2,1,0:T(8,128)(2,1)} %param.5) | copy-start | bytes 4718596
  49.7 5.8 %copy-start.3 = (bf16[4,256,768]{2,1,0:T(8,128)(2,1)S(1)}, bf16[4,256,768]{2,1,0:T(8,128)(2,1)}, u32[]{:S(2)}) copy-start(bf16[4,256,768]{2,1,0:T(8,128)(2,1)} %param.5) | copy-start | bytes 4718596
  49.7 5.8 %copy-start.19 = (bf16[768,768]{1,0:T(8,128)(2,1)S(1)}, bf16[768,768]{1,0:T(8,128)(2,1)}, u32[]{:S(2)}) copy-start(bf16[768,768]{1,0:T(8,128)(2,1)} %param.7) | copy-start | bytes 3538948
  57.1 1.1 copy-start.4
  58.2 44.1 %copy-start.18 = (bf16[768,2304]{1,0:T(8,128)(2,1)S(1)}, bf16[768,2304]{1,0:T(8,128)(2,1)}, u32[]{:S(2)}) copy-start(bf16[768,2304]{1,0:T(8,128)(2,1)} %param.8) | copy-start | bytes 10616836
  147.9 1.4 copy-start.17
  147.9 1.7 copy-start.16
  147.9 1.9 copy-start.15
  148.1 1.9 copy-start.14
  149.3 1.0 copy-start.13
  149.6 1.0 copy-start.12
  149.8 1.0 copy-start.11
  150.1 1.0 copy-start.10
  150.3 1.0 copy-start.9
  150.6 1.0 copy-start.8
  150.8 1.0 copy-start.7
  151.1 1.0 copy-start.6
  193.8 1.4 copy-start.5
  193.8 1.7 copy-start.20
  195.5 2.6 %copy-start.1 = (bf16[768,2304]{1,0:T(8,128)(2,1)S(1)}, bf16[768,2304]{1,0:T(8,128)(2,1)}, u32[]{:S(2)}) copy-start(bf16[768,2304]{1,0:T(8,128)(2,1)} %param.6) | copy-start | bytes 10616836
